TPU v7x, 256 devices: a whole 4x4x8 slice. The times are simulated.
256 devices in a mesh: aux: 32 (over z, x), occ: 8 (over y, core).
Axes of the slice: x: 4, y: 4, z: 8, core: 2. Of those that a mesh axis runs over, the one named last changes fastest.
Arguments:
- half_integrals: float32 [2048, 256, 768], P('aux', 'occ'), may hold values from -2 to 2
- virtual_orbitals: float32 [768, 512], replicated, may hold values from -0.21875 to 0.21875
- occupied_energy: float32 [256], replicated, may hold values from -2 to -0.3
- virtual_energy: float32 [512], replicated, may hold values from 0.3 to 3
- partners: int32 [256, 1], replicated, may hold values from 0 to 255, as said below
Outputs:
- density: float32 [2048, 256, 512], P('aux', 'occ')
Inputs may be any that keep to these rules, and one draw needn't show every extreme that they name: `partners`: occupied orbitals form 8 groups of 32 consecutive ones; of the 32 entries of one group, at most 6 lie in any one group, and exactly 6 in some group.
All inputs are finite; a program needn't handle non-finite values.
Results may differ from a plain program's by a relative error of at most 0.00007.
Values sent between devices are 32-bit elements; how exact they have to be, the bound alone decides.
A program may use at most 128 MiB of HBM per device.

v0:
```python
import jax
import jax.numpy as jnp
from jax import lax
from jax.sharding import PartitionSpec as P


def split_up(array, dim, devices):
    before, after = (array.shape[:dim], array.shape[dim + 1 :])
    return jnp.moveaxis(array.reshape(*before, devices, -1, *after), dim, 0)


def piece_ends(length, count):
    turn = length // count
    if turn >= 8:
        turn -= turn % 8
    return [turn * k for k in range(1, count)]


def in_order(blocks, dim):
    blocks = jnp.moveaxis(blocks, 0, dim)
    lengths = blocks.shape
    return blocks.reshape(*lengths[:dim], lengths[dim] * lengths[dim + 1], *lengths[dim + 2 :])


def exchange_in_pieces(array, axis, pieces, split_dim, concat_dim):
    blocks = split_up(array, split_dim, lax.axis_size(axis))
    split_at = max(range(1, max(2, blocks.ndim - 1)), key=lambda d: blocks.shape[d])
    finished = []
    for share in jnp.split(blocks, piece_ends(blocks.shape[split_at], pieces), axis=split_at):
        if share.size:
            finished.append(lax.all_to_all(share, axis, split_axis=0, concat_axis=0, tiled=True))
    return in_order(jnp.concatenate(finished, axis=split_at), concat_dim)


def local(half_integrals, virtual_orbitals, occupied_energy, virtual_energy, partners):
    highest = lax.Precision.HIGHEST
    groups = lax.axis_size("occ")
    my_group = lax.axis_index("occ")
    my_column = lax.axis_index("aux")
    group_size = half_integrals.shape[1]
    pair_count = partners.shape[1]
    requests = group_size * pair_count
    capacity = requests // groups + 2
    working = jnp.einsum("qim,mv->qiv", half_integrals, virtual_orbitals, precision=highest)
    row_width = working.shape[2]
    slices = working.shape[0]
    source_group = (partners // group_size).reshape(groups, requests)
    local_index = (partners % group_size).reshape(groups, requests)
    request_ids = jnp.arange(requests, dtype=jnp.int32)
    earlier = request_ids[:, None] > request_ids[None, :]
    same_source = source_group[:, :, None] == source_group[:, None, :]
    slot_rank = jnp.sum((same_source & earlier[None]).astype(jnp.int32), axis=2)
    outgoing = (source_group == my_group).astype(jnp.int32)
    slot_ids = jnp.arange(capacity, dtype=jnp.int32)
    slot_match = outgoing[:, None, :] * (slot_rank[:, None, :] == slot_ids[None, :, None]).astype(
        jnp.int32
    )
    chosen = jnp.sum(slot_match * local_index[:, None, :], axis=2).reshape(-1)
    filled = jnp.sum(slot_match, axis=2).reshape(-1)
    outbound = jnp.take(working, chosen, axis=1) * filled.astype(working.dtype)[None, :, None]
    outbound = outbound.reshape(slices, groups, capacity, row_width)
    inbound = lax.all_to_all(outbound, "occ", split_axis=1, concat_axis=1, tiled=True)
    my_sources = lax.dynamic_index_in_dim(source_group, my_group, 0, keepdims=False)
    my_ranks = lax.dynamic_index_in_dim(slot_rank, my_group, 0, keepdims=False)
    partner_rows = jnp.take(
        inbound.reshape(slices, groups * capacity, row_width),
        my_sources * capacity + my_ranks,
        axis=1,
    )
    partner_rows = partner_rows.reshape(slices, group_size, pair_count, row_width)
    per_device = group_size // lax.axis_size("aux")
    first_orbital = my_group * group_size + my_column * per_device
    own_energy = lax.dynamic_slice_in_dim(occupied_energy, first_orbital, per_device, 0)
    own_partners = lax.dynamic_slice_in_dim(partners, first_orbital, per_device, 0)
    orbital_ids = jnp.arange(occupied_energy.shape[0], dtype=jnp.int32)
    partner_energy = jnp.sum(
        jnp.where(
            own_partners[:, :, None] == orbital_ids[None, None, :],
            occupied_energy[None, None, :],
            jnp.float32(0.0),
        ),
        axis=2,
    )
    pair_energy = (
        jnp.concatenate([own_energy[:, None], partner_energy], axis=1) + own_energy[:, None]
    )
    denominator = (
        virtual_energy[None, None, :, None]
        + virtual_energy[None, None, None, :]
        - pair_energy[:, :, None, None]
    )
    own_rows = exchange_in_pieces(working, "aux", 2, 1, 0)
    self_ints = jnp.einsum("qda,qdb->dab", own_rows, own_rows, precision=highest)
    self_amplitude = self_ints / denominator[:, 0]
    self_term = jnp.einsum("dab,qdb->qda", self_amplitude, own_rows, precision=highest)
    member_rows = lax.all_to_all(partner_rows, "aux", split_axis=1, concat_axis=0, tiled=True)
    cross_ints = jnp.einsum("qda,qdkb->dkab", own_rows, member_rows, precision=highest)
    cross_amplitude = cross_ints / denominator[:, 1:]
    gathered = self_term + jnp.einsum(
        "dkab,qdkb->qda", cross_amplitude, member_rows, precision=highest
    )
    return lax.all_to_all(gathered, "aux", split_axis=0, concat_axis=1, tiled=True)


def solution(mesh):
    return jax.shard_map(
        local,
        mesh=mesh,
        in_specs=(P("aux", "occ", None), P(), P(), P(), P()),
        out_specs=P("aux", "occ", None),
        check_vma=False,
    )
```

profile of v0, /device:TPU:2, one launch (start us, length us, event | category | flops | bytes accessed | tf_op | source)
XLA Modules:
  0.0 455.3 jit_solution(16977519400593986430)
XLA Ops:
  0.0 0.0 copy-start
  0.0 1.4 copy-done
  1.4 12.3 %fusion.3 = f32[64,32,512]{2,1,0:T(8,128)S(1)} fusion(f32[64,32,768]{2,1,0:T(8,128)} %param.5, f32[768,512]{1,0:T(8,128)S(1)} %copy-done), kind=kOutput, calls=%fused_computation.11 | convolution fusion | flops 9663676416 | bytes 12058624 | tf_op jit(solution)/shard_map/qim,mv->qiv/dot_general | solution.py:44
  13.7 0.0 copy-start.3
  13.7 2.3 fusion.22
  16.1 0.3 copy-done.3
  16.4 2.5 copy.20
  18.9 11.7 %all-to-all-start = ((f32[32,32,1,512]{3,1,2,0:T(8,128)}), f32[32,32,1,512]{3,1,2,0:T(8,128)}, u32[]{:S(2)}, u32[]{:S(2)}) async-start(f32[32,32,1,512]{3,1,2,0:T(8,128)} %copy.20), calls=%async_computation | async-start | bytes 4194304 | tf_op jit(solution)/shard_map/all_to_all | solution.py:31
  30.6 0.0 copy-start.7
  30.6 6.6 %copy.27 = f32[64,32,512]{2,0,1:T(8,128)} copy(f32[64,32,512]{2,1,0:T(8,128)} %copy-done.3) | data formatting | bytes 8388608 | tf_op jit(solution)/shard_map/qim,mv->qiv/dot_general | solution.py:44
  37.2 0.0 copy-done.7
  37.2 0.1 reshape.243
  37.3 0.1 mul.52
  37.4 0.3 convert_reduce_fusion
  37.7 0.3 select_reduce_fusion
  38.0 0.1 copy.26
  38.1 0.1 reshape.244
  38.2 0.1 copy.25
  38.3 0.1 copy.28
  38.4 5.8 %gather_fusion = f32[48,64,512]{2,1,0:T(8,128)} fusion(f32[64,32,512]{2,0,1:T(8,128)} %copy.27, s32[1024]{0:T(1024)S(1)} %pad_clamp_fusion.1), kind=kCustom, calls=%fused_computation | custom fusion | bytes 12583104 | tf_op jit(solution)/shard_map/jit(_take)/gather | solution.py:60
  44.2 6.9 %select_multiply_fusion = f32[64,8,6,512]{3,0,2,1:T(8,128)} fusion(f32[64,8,6,512]{3,0,2,1:T(8,128)} %bitcast.78, f32[8,6]{1,0:T(8,128)S(1)} %copy.28, pred[8,6]{1,0:T(8,128)(4,1)S(1)} %copy.25), kind=kLoop, calls=%fused_computation.2 | loop fusion | flops 3145728 | bytes 12583152 | tf_op jit(solution)/shard_map/mul | solution.py:60
  51.1 28.8 %all-to-all-done = f32[32,32,1,512]{3,1,2,0:T(8,128)} async-done(((f32[32,32,1,512]{3,1,2,0:T(8,128)}), f32[32,32,1,512]{3,1,2,0:T(8,128)}, u32[]{:S(2)}, u32[]{:S(2)}) %all-to-all-start) | async-done | bytes 2097184 | tf_op jit(solution)/shard_map/all_to_all | solution.py:31
  79.9 15.5 %all-to-all-start.2 = ((f32[64,8,6,512]{3,0,2,1:T(8,128)}), f32[64,8,6,512]{3,0,2,1:T(8,128)}, u32[]{:S(2)}, u32[]{:S(2)}) async-start(f32[64,8,6,512]{3,0,2,1:T(8,128)} %select_multiply_fusion), calls=%async_computation.2 | async-start | bytes 12582912 | tf_op jit(solution)/shard_map/all_to_all | solution.py:62
  95.4 4.1 copy.21
  99.5 68.0 %all-to-all-done.2 = f32[64,8,6,512]{3,0,2,1:T(8,128)} async-done(((f32[64,8,6,512]{3,0,2,1:T(8,128)}), f32[64,8,6,512]{3,0,2,1:T(8,128)}, u32[]{:S(2)}, u32[]{:S(2)}) %all-to-all-start.2) | async-done | bytes 6291488 | tf_op jit(solution)/shard_map/all_to_all | solution.py:62
  167.5 6.9 %all-to-all-start.1 = ((f32[32,32,1,512]{3,1,2,0:T(8,128)}), f32[32,32,1,512]{3,1,2,0:T(8,128)}, u32[]{:S(2)}, u32[]{:S(2)}) async-start(f32[32,32,1,512]{3,1,2,0:T(8,128)} %copy.21), calls=%async_computation.1 | async-start | bytes 4194304 | tf_op jit(solution)/shard_map/all_to_all | solution.py:31
  174.5 5.6 %gather_fusion.1 = f32[32,64,512]{2,1,0:T(8,128)} fusion(f32[64,48,512]{2,0,1:T(8,128)} %bitcast.15, s32[1024]{0:T(1024)S(1)} %pad_clamp_fusion), kind=kCustom, calls=%fused_computation.1 | custom fusion | bytes 8388736 | tf_op jit(solution)/shard_map/jit(_take)/gather | solution.py:65
  180.1 5.0 %fusion = f32[64,32,1,512]{3,0,2,1:T(8,128)} fusion(f32[32,64,512]{2,1,0:T(8,128)} %gather_fusion.1, pred[32]{0:T(512)(128)(4,1)S(1)} %get-tuple-element.9), kind=kLoop, calls=%fused_computation.4 | loop fusion | flops 1048576 | bytes 8388640 | tf_op jit(solution)/shard_map/jit(_take)/select_n | solution.py:65
  185.1 38.5 %all-to-all-done.1 = f32[32,32,1,512]{3,1,2,0:T(8,128)} async-done(((f32[32,32,1,512]{3,1,2,0:T(8,128)}), f32[32,32,1,512]{3,1,2,0:T(8,128)}, u32[]{:S(2)}, u32[]{:S(2)}) %all-to-all-start.1) | async-done | bytes 2097184 | tf_op jit(solution)/shard_map/all_to_all | solution.py:31
  223.6 6.9 %all-to-all-start.3 = ((f32[64,32,1,512]{3,0,2,1:T(8,128)}), f32[64,32,1,512]{3,0,2,1:T(8,128)}, u32[]{:S(2)}, u32[]{:S(2)}) async-start(f32[64,32,1,512]{3,0,2,1:T(8,128)} %fusion), calls=%async_computation.3 | async-start | bytes 8388608 | tf_op jit(solution)/shard_map/all_to_all | solution.py:96
  230.5 0.6 constant_dynamic-slice_fusion.2
  231.0 0.6 dynamic_slice.13
  231.7 1.2 fusion.14
  232.9 2.0 maximum_add_fusion
  234.9 0.1 broadcast_add_fusion
  235.0 0.3 broadcast_subtract_fusion
  235.4 3.6 copy_dynamic-update-slice_fusion.1
  238.9 2.8 copy_dynamic-update-slice_fusion
  241.7 2.4 copy.24
  244.2 7.0 %fusion.8 = f32[512,512]{1,0:T(8,128)S(1)} fusion(f32[32,64,1,512]{3,0,1,2:T(8,128)S(1)} %copy_dynamic-update-slice_fusion, f32[1,2,512,512]{3,2,1,0:T(8,128)S(1)} %broadcast_subtract_fusion), kind=kOutput, calls=%fused_computation.15 | convolution fusion | flops 6442713088 | bytes 6291456 | tf_op jit(solution)/shard_map/qda,qdb->dab/dot_general | solution.py:93
  251.2 0.0 copy-done.2
  251.2 8.3 %fusion.23 = f32[2048,512]{1,0:T(8,128)} fusion(f32[2048,512]{1,0:T(8,128)S(1)} %bitcast.75, f32[512,512]{1,0:T(8,128)S(1)} %fusion.8), kind=kOutput, calls=%fused_computation.54 | convolution fusion | flops 6442450944 | bytes 9437184 | tf_op jit(solution)/shard_map/dab,qdb->qda/dot_general | solution.py:95
  259.5 63.2 %all-to-all-done.3 = f32[64,32,1,512]{3,0,2,1:T(8,128)} async-done(((f32[64,32,1,512]{3,0,2,1:T(8,128)}), f32[64,32,1,512]{3,0,2,1:T(8,128)}, u32[]{:S(2)}, u32[]{:S(2)}) %all-to-all-start.3) | async-done | bytes 4194336 | tf_op jit(solution)/shard_map/all_to_all | solution.py:96
  322.7 9.9 %fusion.12 = f32[512,512]{1,0:T(8,128)S(1)} fusion(f32[2048,512]{1,0:T(8,128)} %bitcast.23, f32[2048,512]{1,0:T(8,128)} %bitcast.76, f32[1,2,512,512]{3,2,1,0:T(8,128)} %copy-done.5), kind=kOutput, calls=%fused_computation.17 | convolution fusion | flops 6442713088 | bytes 10485760 | tf_op jit(solution)/shard_map/qda,qdkb->dkab/dot_general | solution.py:97
  332.6 8.6 %add_bitcast_fusion = f32[2048,1,512]{2,0,1:T(8,128)S(1)} fusion(f32[2048,512]{1,0:T(8,128)S(1)} %copy-done.4, f32[2048,512]{1,0:T(8,128)} %bitcast.23, f32[512,512]{1,0:T(8,128)S(1)} %fusion.12), kind=kOutput, calls=%fused_computation.8 | convolution fusion | flops 6443499520 | bytes 13631488 | tf_op jit(solution)/shard_map/dkab,qdkb->qda/dot_general | solution.py:99
  341.2 8.0 %copy.31 = f32[2048,1,512]{2,1,0:T(1,128)S(1)} copy(f32[2048,1,512]{2,0,1:T(8,128)S(1)} %add_bitcast_fusion) | data formatting | bytes 8388608 | tf_op jit(solution)/shard_map/add | solution.py:99
  349.2 101.2 %all_to_all.48 = f32[2048,1,512]{2,1,0:T(1,128)S(1)} all-to-all(f32[2048,1,512]{2,1,0:T(1,128)S(1)} %copy.31), channel_id=1, replica_groups=mesh['aux'=32,'occ'=8] {'aux'}, dimensions={0} | all-to-all | bytes 8388608 | tf_op jit(solution)/shard_map/all_to_all | solution.py:102
  450.4 4.4 copy.37
  (21 shorter events, 0.1 us)
Async XLA Ops:
  0.0 1.4 copy-start
  13.7 2.7 copy-start.3
  18.9 61.0 %all-to-all-start = ((f32[32,32,1,512]{3,1,2,0:T(8,128)}), f32[32,32,1,512]{3,1,2,0:T(8,128)}, u32[]{:S(2)}, u32[]{:S(2)}) async-start(f32[32,32,1,512]{3,1,2,0:T(8,128)} %copy.20), calls=%async_computation | async-start | bytes 4194304 | tf_op jit(solution)/shard_map/all_to_all | solution.py:31
  30.6 6.6 %copy-start.7 = (s32[256,1]{0,1:T(1,128)S(1)}, s32[256,1]{0,1:T(1,128)}, u32[]{:S(2)}) copy-start(s32[256,1]{0,1:T(1,128)} %param.9) | copy-start | bytes 3076
  79.9 87.6 %all-to-all-start.2 = ((f32[64,8,6,512]{3,0,2,1:T(8,128)}), f32[64,8,6,512]{3,0,2,1:T(8,128)}, u32[]{:S(2)}, u32[]{:S(2)}) async-start(f32[64,8,6,512]{3,0,2,1:T(8,128)} %select_multiply_fusion), calls=%async_computation.2 | async-start | bytes 12582912 | tf_op jit(solution)/shard_map/all_to_all | solution.py:62
  167.5 56.0 %all-to-all-start.1 = ((f32[32,32,1,512]{3,1,2,0:T(8,128)}), f32[32,32,1,512]{3,1,2,0:T(8,128)}, u32[]{:S(2)}, u32[]{:S(2)}) async-start(f32[32,32,1,512]{3,1,2,0:T(8,128)} %copy.21), calls=%async_computation.1 | async-start | bytes 4194304 | tf_op jit(solution)/shard_map/all_to_all | solution.py:31
  185.1 46.0 %copy-start.8 = (f32[256]{0:T(256)S(1)}, f32[256]{0:T(256)}, u32[]{:S(2)}) copy-start(f32[256]{0:T(256)} %param.7) | copy-start | bytes 3076
  185.1 49.8 %copy-start.6 = (f32[512]{0:T(512)S(1)}, f32[512]{0:T(512)}, u32[]{:S(2)}) copy-start(f32[512]{0:T(512)} %param.8) | copy-start | bytes 6148
  223.6 99.2 %all-to-all-start.3 = ((f32[64,32,1,512]{3,0,2,1:T(8,128)}), f32[64,32,1,512]{3,0,2,1:T(8,128)}, u32[]{:S(2)}, u32[]{:S(2)}) async-start(f32[64,32,1,512]{3,0,2,1:T(8,128)} %fusion), calls=%async_computation.3 | async-start | bytes 8388608 | tf_op jit(solution)/shard_map/all_to_all | solution.py:96
  235.4 8.8 %copy-start.5 = (f32[1,2,512,512]{3,2,1,0:T(8,128)}, f32[1,2,512,512]{3,2,1,0:T(8,128)S(1)}, u32[]{:S(2)}) copy-start(f32[1,2,512,512]{3,2,1,0:T(8,128)S(1)} %broadcast_subtract_fusion) | copy-start | bytes 6291460
  244.2 7.0 %copy-start.2 = (f32[32,64,1,512]{3,1,0,2:T(8,128)}, f32[32,64,1,512]{3,1,0,2:T(8,128)S(1)}, u32[]{:S(2)}) copy-start(f32[32,64,1,512]{3,1,0,2:T(8,128)S(1)} %copy.24) | copy-start | bytes 12582916
  322.7 9.9 %copy-start.4 = (f32[2048,512]{1,0:T(8,128)S(1)}, f32[2048,512]{1,0:T(8,128)}, u32[]{:S(2)}) copy-start(f32[2048,512]{1,0:T(8,128)} %fusion.23) | copy-start | bytes 12582916
  450.4 4.4 copy-start.1
where the time goes:
time: 464 us; the launch traced here: 455 us
  waiting for transfers between devices  199 us (43%)
  blocking collectives  101 us (22%)
  local copies, waits for them, and re-layouts  51.8 us (11%)
  matrix products  46 us (10%)
  starting transfers between devices  40.9 us (9%)
  other arithmetic  16.2 us (3%)
    all_to_all x1, blocking collectives, local(): lax.all_to_all(gathered, 'aux', split_axis=0, concat_axis=1, tiled=True)  101 us
    all_to_all x1, waiting for transfers between devices, local(): lax.all_to_all(outbound, 'occ', split_axis=1, concat_axis=1, tiled=True)  68 us
    all_to_all x2, waiting for transfers between devices, exchange_in_pieces(): lax.all_to_all(share, axis, split_axis=0, concat_axis=0, tiled=True)  67.3 us
    all_to_all x1, waiting for transfers between devices, local(): lax.all_to_all(partner_rows, 'aux', split_axis=1, concat_axis=0, tiled=True)  63.2 us
    all_to_all x2, starting transfers between devices, exchange_in_pieces(): lax.all_to_all(share, axis, split_axis=0, concat_axis=0, tiled=True)  18.6 us
    all_to_all x1, starting transfers between devices, local(): lax.all_to_all(outbound, 'occ', split_axis=1, concat_axis=1, tiled=True)  15.5 us
    dot_general x1, matrix products, local(): jnp.einsum('qim,mv->qiv', half_integrals, virtual_orbitals, precision=hig...  12.3 us
    dot_general x1, matrix products, local(): jnp.einsum('qda,qdkb->dkab', own_rows, member_rows, precision=highest)  9.86 us
  transfers between devices with their start and end apart: 4, of which 4 were waited for; matrix products, arithmetic and copies ran while one was open for 14% of the time, Pallas kernels for 0%

commit v1 on v0

--- a/solution.py
+++ b/solution.py
@@ -2,6 +2,21 @@
 import jax.numpy as jnp
 from jax import lax
 from jax.sharding import PartitionSpec as P
+from jax.lax import axis_index, axis_size, ppermute
+
+
+def kinds_process(field, at_axis, x_local):
+    v_next = field.shape
+    everything = field.reshape(
+        *v_next[:at_axis], x_local, v_next[at_axis] // x_local, *v_next[at_axis + 1 :]
+    )
+    return jnp.moveaxis(everything, at_axis, 0)
+
+
+def do_the_squares(array_here, d0):
+    array_here = jnp.moveaxis(array_here, 0, d0)
+    w2 = array_here.shape
+    return array_here.reshape(*w2[:d0], w2[d0] * w2[d0 + 1], *w2[d0 + 2 :])
 
 
 def split_up(array, dim, devices):
@@ -59,7 +74,20 @@
     filled = jnp.sum(slot_match, axis=2).reshape(-1)
     outbound = jnp.take(working, chosen, axis=1) * filled.astype(working.dtype)[None, :, None]
     outbound = outbound.reshape(slices, groups, capacity, row_width)
-    inbound = lax.all_to_all(outbound, "occ", split_axis=1, concat_axis=1, tiled=True)
+    newest = axis_size("occ")
+    moved = axis_index("occ")
+    current_block, k_now = (newest, moved)
+    current_value = kinds_process(outbound, 1, current_block)
+    slots = [current_value[k_now]]
+    for ix in range(1, current_block):
+        piece_now = current_value[k_now ^ ix]
+        mat_out = ppermute(
+            piece_now, "occ", [(dev_j, dev_j ^ ix) for dev_j in range(current_block)]
+        )
+        slots.append(mat_out)
+    y2 = jnp.stack(slots, axis=0)
+    current_value = y2[k_now ^ jnp.arange(current_block)]
+    inbound = do_the_squares(current_value, 1)
     my_sources = lax.dynamic_index_in_dim(source_group, my_group, 0, keepdims=False)
     my_ranks = lax.dynamic_index_in_dim(slot_rank, my_group, 0, keepdims=False)
     partner_rows = jnp.take(

time: 464 us -> 447 us (0.963)
  waiting for transfers between devices: 199 us -> 173 us
  local copies, waits for them, and re-layouts: 51.8 us -> 66.5 us
    all_to_all x1 -> x0, waiting for transfers between devices: 68 us -> none  [local(): lax.all_to_all(outbound, 'occ', split_axis=1, concat_axis=1, tiled=True)]
    ppermute x0 -> x7, waiting for transfers between devices: none -> 60.7 us  [local(): ppermute(piece_now, 'occ', [(dev_j, dev_j ^ ix) for dev_j in range(curren...]
    all_to_all x2, waiting for transfers between devices: 67.3 us -> 44.1 us  [exchange_in_pieces(): lax.all_to_all(share, axis, split_axis=0, concat_axis=0, tiled=True)]
    all_to_all x1 -> x0, starting transfers between devices: 15.5 us -> none  [local(): lax.all_to_all(outbound, 'occ', split_axis=1, concat_axis=1, tiled=True)]
    ppermute x0 -> x7, starting transfers between devices: none -> 10.1 us  [local(): ppermute(piece_now, 'occ', [(dev_j, dev_j ^ ix) for dev_j in range(curren...]
    unnamed x19 -> x26, local copies, waits for them, and re-layouts: 5.35 us -> 12.1 us
    gather x0 -> x1, local copies, waits for them, and re-layouts: none -> 6.39 us  [local(): current_value = y2[k_now ^ jnp.arange(current_block)]]
    all_to_all x1, waiting for transfers between devices: 63.2 us -> 68.4 us  [local(): lax.all_to_all(partner_rows, 'aux', split_axis=1, concat_axis=0, tiled=True)]
  transfers between devices with their start and end apart: 4 -> 10, of which waited for: 4 -> 7; matrix products, arithmetic and copies ran while one was open for 14% -> 17% of each run, Pallas kernels for 0% -> 0%
where the time goes in v1:
time: 447 us; the launch traced here: 439 us
  waiting for transfers between devices  173 us (39%)
  blocking collectives  100 us (22%)
  local copies, waits for them, and re-layouts  66.5 us (15%)
  matrix products  46 us (10%)
  starting transfers between devices  39.5 us (9%)
  other arithmetic  13.3 us (3%)
    all_to_all x1, blocking collectives, local(): lax.all_to_all(gathered, 'aux', split_axis=0, concat_axis=1, tiled=True)  100 us
    all_to_all x1, waiting for transfers between devices, local(): lax.all_to_all(partner_rows, 'aux', split_axis=1, concat_axis=0, tiled=True)  68.4 us
    ppermute x7, waiting for transfers between devices, local(): ppermute(piece_now, 'occ', [(dev_j, dev_j ^ ix) for dev_j in range(curren...  60.7 us
    all_to_all x2, waiting for transfers between devices, exchange_in_pieces(): lax.all_to_all(share, axis, split_axis=0, concat_axis=0, tiled=True)  44.1 us
    all_to_all x2, starting transfers between devices, exchange_in_pieces(): lax.all_to_all(share, axis, split_axis=0, concat_axis=0, tiled=True)  19.3 us
    dot_general x1, matrix products, local(): jnp.einsum('qim,mv->qiv', half_integrals, virtual_orbitals, precision=hig...  12.3 us
    unnamed x26, local copies, waits for them, and re-layouts  12.1 us
    all_to_all x1, starting transfers between devices, local(): lax.all_to_all(partner_rows, 'aux', split_axis=1, concat_axis=0, tiled=True)  10.1 us
  transfers between devices with their start and end apart: 10, of which 7 were waited for; matrix products, arithmetic and copies ran while one was open for 17% of the time, Pallas kernels for 0%

profile of v1, /device:TPU:2, one launch (start us, length us, event | category | flops | bytes accessed | tf_op | source)
XLA Modules:
  0.0 439.2 jit_solution(4263117590002673382)
XLA Ops:
  0.0 1.4 copy-done
  1.4 12.3 %fusion.3 = f32[64,32,512]{2,1,0:T(8,128)S(1)} fusion(f32[64,32,768]{2,1,0:T(8,128)} %param.5, f32[768,512]{1,0:T(8,128)S(1)} %copy-done), kind=kOutput, calls=%fused_computation.12 | convolution fusion | flops 9663676416 | bytes 12058624 | tf_op jit(solution)/shard_map/qim,mv->qiv/dot_general | solution.py:59
  13.7 2.3 fusion.23
  16.4 2.6 copy.20
  18.9 11.7 %all-to-all-start = ((f32[32,32,1,512]{3,1,2,0:T(8,128)}), f32[32,32,1,512]{3,1,2,0:T(8,128)}, u32[]{:S(2)}, u32[]{:S(2)}) async-start(f32[32,32,1,512]{3,1,2,0:T(8,128)} %copy.20), calls=%async_computation | async-start | bytes 4194304 | tf_op jit(solution)/shard_map/all_to_all | solution.py:46
  31.6 4.2 copy.21
  35.8 44.1 %all-to-all-done = f32[32,32,1,512]{3,1,2,0:T(8,128)} async-done(((f32[32,32,1,512]{3,1,2,0:T(8,128)}), f32[32,32,1,512]{3,1,2,0:T(8,128)}, u32[]{:S(2)}, u32[]{:S(2)}) %all-to-all-start) | async-done | bytes 2097184 | tf_op jit(solution)/shard_map/all_to_all | solution.py:46
  79.9 7.6 %all-to-all-start.1 = ((f32[32,32,1,512]{3,1,2,0:T(8,128)}), f32[32,32,1,512]{3,1,2,0:T(8,128)}, u32[]{:S(2)}, u32[]{:S(2)}) async-start(f32[32,32,1,512]{3,1,2,0:T(8,128)} %copy.21), calls=%async_computation.1 | async-start | bytes 4194304 | tf_op jit(solution)/shard_map/all_to_all | solution.py:46
  87.6 6.6 %copy.27 = f32[64,32,512]{2,0,1:T(8,128)} copy(f32[64,32,512]{2,1,0:T(8,128)} %copy-done.3) | data formatting | bytes 8388608 | tf_op jit(solution)/shard_map/qim,mv->qiv/dot_general | solution.py:59
  94.4 5.8 %gather_fusion = f32[48,64,512]{2,1,0:T(8,128)} fusion(f32[64,32,512]{2,0,1:T(8,128)} %copy.27, s32[1024]{0:T(1024)S(1)} %get-tuple-element.21), kind=kCustom, calls=%fused_computation | custom fusion | bytes 12583104 | tf_op jit(solution)/shard_map/jit(_take)/gather | solution.py:75
  100.2 4.1 select_multiply_fusion
  104.3 0.6 dynamic-slice_bitcast_fusion
  105.0 1.7 collective-permute-start.1
  106.9 3.2 collective-permute-start.3
  110.1 1.0 bitcast_dynamic-update-slice_fusion.7
  111.1 3.0 collective-permute-start.5
  114.1 1.0 bitcast_dynamic-update-slice_fusion.6
  115.1 10.4 %collective-permute-done.1 = f32[64,1,6,512]{3,0,2,1:T(8,128)S(1)} collective-permute-done((f32[64,1,6,512]{3,0,2,1:T(8,128)S(1)}, f32[64,1,6,512]{3,0,2,1:T(8,128)S(1)}, u32[]{:S(2)}, u32[]{:S(2)}) %collective-permute-start.1) | collective-permute-done | bytes 786464 | tf_op jit(solution)/shard_map/ppermute | solution.py:84
  125.4 1.9 collective-permute-start.6
  127.3 0.9 bitcast_dynamic-update-slice_fusion.5
  128.2 13.1 %collective-permute-done.2 = f32[64,1,6,512]{3,0,2,1:T(8,128)S(1)} collective-permute-done((f32[64,1,6,512]{3,0,2,1:T(8,128)S(1)}, f32[64,1,6,512]{3,0,2,1:T(8,128)S(1)}, u32[]{:S(2)}, u32[]{:S(2)}) %collective-permute-start.2) | collective-permute-done | bytes 786464 | tf_op jit(solution)/shard_map/ppermute | solution.py:84
  141.4 0.9 bitcast_dynamic-update-slice_fusion.4
  142.3 19.4 %collective-permute-done.3 = f32[64,1,6,512]{3,0,2,1:T(8,128)S(1)} collective-permute-done((f32[64,1,6,512]{3,0,2,1:T(8,128)S(1)}, f32[64,1,6,512]{3,0,2,1:T(8,128)S(1)}, u32[]{:S(2)}, u32[]{:S(2)}) %collective-permute-start.3) | collective-permute-done | bytes 786464 | tf_op jit(solution)/shard_map/ppermute | solution.py:84
  161.7 0.9 bitcast_dynamic-update-slice_fusion.3
  162.6 15.0 %collective-permute-done.4 = f32[64,1,6,512]{3,0,2,1:T(8,128)S(1)} collective-permute-done((f32[64,1,6,512]{3,0,2,1:T(8,128)S(1)}, f32[64,1,6,512]{3,0,2,1:T(8,128)S(1)}, u32[]{:S(2)}, u32[]{:S(2)}) %collective-permute-start.4) | collective-permute-done | bytes 786464 | tf_op jit(solution)/shard_map/ppermute | solution.py:84
  177.6 1.0 bitcast_dynamic-update-slice_fusion.2
  178.6 1.0 bitcast_dynamic-update-slice_fusion.1
  179.6 2.8 collective-permute-done.6
  182.4 1.0 bitcast_dynamic-update-slice_fusion
  183.4 6.4 %gather_fusion.1 = f32[8,64,6,512]{3,1,2,0:T(8,128)} fusion(f32[8,64,6,512]{3,1,2,0:T(8,128)} %bitcast.30, s32[1024]{0:T(1024)S(1)} %pad_clamp_fusion.1), kind=kCustom, calls=%fused_computation.1 | custom fusion | bytes 12582944 | tf_op jit(solution)/shard_map/gather | solution.py:89
  189.8 5.6 %gather_fusion.2 = f32[32,64,512]{2,1,0:T(8,128)} fusion(f32[64,48,512]{2,0,1:T(8,128)} %bitcast.116, s32[1024]{0:T(1024)S(1)} %get-tuple-element.20), kind=kCustom, calls=%fused_computation.2 | custom fusion | bytes 8388736 | tf_op jit(solution)/shard_map/jit(_take)/gather | solution.py:93
  195.4 5.0 %fusion = f32[64,32,1,512]{3,0,2,1:T(8,128)} fusion(f32[32,64,512]{2,1,0:T(8,128)} %gather_fusion.2, pred[32]{0:T(512)(128)(4,1)S(1)} %get-tuple-element.9), kind=kLoop, calls=%fused_computation.5 | loop fusion | flops 1048576 | bytes 8388640 | tf_op jit(solution)/shard_map/jit(_take)/select_n | solution.py:93
  200.4 10.1 %all-to-all-start.2 = ((f32[64,32,1,512]{3,0,2,1:T(8,128)}), f32[64,32,1,512]{3,0,2,1:T(8,128)}, u32[]{:S(2)}, u32[]{:S(2)}) async-start(f32[64,32,1,512]{3,0,2,1:T(8,128)} %fusion), calls=%async_computation.2 | async-start | bytes 8388608 | tf_op jit(solution)/shard_map/all_to_all | solution.py:124
  210.5 0.6 constant_dynamic-slice_fusion.2
  211.1 0.6 dynamic_slice.23
  211.7 1.3 fusion.14
  213.0 1.8 maximum_add_fusion
  215.3 3.6 copy_dynamic-update-slice_fusion.1
  218.9 2.8 copy_dynamic-update-slice_fusion
  221.7 2.4 copy.24
  224.1 7.0 %fusion.8 = f32[512,512]{1,0:T(8,128)S(1)} fusion(f32[32,64,1,512]{3,0,1,2:T(8,128)S(1)} %copy_dynamic-update-slice_fusion, f32[1,2,512,512]{3,2,1,0:T(8,128)S(1)} %broadcast_subtract_fusion), kind=kOutput, calls=%fused_computation.16 | convolution fusion | flops 6442713088 | bytes 6291456 | tf_op jit(solution)/shard_map/qda,qdb->dab/dot_general | solution.py:121
  231.2 8.3 %fusion.24 = f32[2048,512]{1,0:T(8,128)} fusion(f32[2048,512]{1,0:T(8,128)S(1)} %bitcast.112, f32[512,512]{1,0:T(8,128)S(1)} %fusion.8), kind=kOutput, calls=%fused_computation.73 | convolution fusion | flops 6442450944 | bytes 9437184 | tf_op jit(solution)/shard_map/dab,qdb->qda/dot_general | solution.py:123
  239.5 68.4 %all-to-all-done.2 = f32[64,32,1,512]{3,0,2,1:T(8,128)} async-done(((f32[64,32,1,512]{3,0,2,1:T(8,128)}), f32[64,32,1,512]{3,0,2,1:T(8,128)}, u32[]{:S(2)}, u32[]{:S(2)}) %all-to-all-start.2) | async-done | bytes 4194336 | tf_op jit(solution)/shard_map/all_to_all | solution.py:124
  307.9 9.9 %fusion.12 = f32[512,512]{1,0:T(8,128)S(1)} fusion(f32[2048,512]{1,0:T(8,128)} %bitcast.42, f32[2048,512]{1,0:T(8,128)} %bitcast.113, f32[1,2,512,512]{3,2,1,0:T(8,128)} %copy-done.5), kind=kOutput, calls=%fused_computation.18 | convolution fusion | flops 6442713088 | bytes 10485760 | tf_op jit(solution)/shard_map/qda,qdkb->dkab/dot_general | solution.py:125
  317.8 8.6 %add_bitcast_fusion = f32[2048,1,512]{2,0,1:T(8,128)S(1)} fusion(f32[2048,512]{1,0:T(8,128)S(1)} %copy-done.4, f32[2048,512]{1,0:T(8,128)} %bitcast.42, f32[512,512]{1,0:T(8,128)S(1)} %fusion.12), kind=kOutput, calls=%fused_computation.9 | convolution fusion | flops 6443499520 | bytes 13631488 | tf_op jit(solution)/shard_map/dkab,qdkb->qda/dot_general | solution.py:127
  326.3 8.0 %copy.31 = f32[2048,1,512]{2,1,0:T(1,128)S(1)} copy(f32[2048,1,512]{2,0,1:T(8,128)S(1)} %add_bitcast_fusion) | data formatting | bytes 8388608 | tf_op jit(solution)/shard_map/add | solution.py:127
  334.3 100.0 %all_to_all.43 = f32[2048,1,512]{2,1,0:T(1,128)S(1)} all-to-all(f32[2048,1,512]{2,1,0:T(1,128)S(1)} %copy.31), channel_id=1, replica_groups=mesh['aux'=32,'occ'=8] {'aux'}, dimensions={0} | all-to-all | bytes 8388608 | tf_op jit(solution)/shard_map/all_to_all | solution.py:130
  434.3 4.4 %copy.37 = f32[32,64,1,512]{3,0,1,2:T(8,128)} copy(f32[32,64,1,512]{3,2,1,0:T(1,128)S(1)} %bitcast.117) | data formatting | bytes 8388608 | tf_op jit(solution)/shard_map/all_to_all | solution.py:130
  (44 shorter events, 2.3 us)
Async XLA Ops:
  0.0 1.4 copy-start
  13.7 2.7 copy-start.3
  16.4 14.2 %copy-start.7 = (s32[256,1]{0,1:T(1,128)S(1)}, s32[256,1]{0,1:T(1,128)}, u32[]{:S(2)}) copy-start(s32[256,1]{0,1:T(1,128)} %param.9) | copy-start | bytes 3076
  18.9 61.0 %all-to-all-start = ((f32[32,32,1,512]{3,1,2,0:T(8,128)}), f32[32,32,1,512]{3,1,2,0:T(8,128)}, u32[]{:S(2)}, u32[]{:S(2)}) async-start(f32[32,32,1,512]{3,1,2,0:T(8,128)} %copy.20), calls=%async_computation | async-start | bytes 4194304 | tf_op jit(solution)/shard_map/all_to_all | solution.py:46
  79.9 120.4 %all-to-all-start.1 = ((f32[32,32,1,512]{3,1,2,0:T(8,128)}), f32[32,32,1,512]{3,1,2,0:T(8,128)}, u32[]{:S(2)}, u32[]{:S(2)}) async-start(f32[32,32,1,512]{3,1,2,0:T(8,128)} %copy.21), calls=%async_computation.1 | async-start | bytes 4194304 | tf_op jit(solution)/shard_map/all_to_all | solution.py:46
  104.9 6.2 %collective-permute-start = (f32[64,1,6,512]{3,0,2,1:T(8,128)S(1)}, f32[64,1,6,512]{3,0,2,1:T(8,128)S(1)}, u32[]{:S(2)}, u32[]{:S(2)}) collective-permute-start(f32[64,1,6,512]{3,0,2,1:T(8,128)S(1)} %get-tuple-element.17), channel_id=1, source_target_pairs={{0,1},{1,0},{2,3},{3,2},{4,5},{5,4},{6,7},{7,6},{8,9},{9,8},{10,11... | collective-permute-start | bytes 2359304 | tf_op jit(solution)/shard_map/ppermute | solution.py:84
  105.0 20.4 %collective-permute-start.1 = (f32[64,1,6,512]{3,0,2,1:T(8,128)S(1)}, f32[64,1,6,512]{3,0,2,1:T(8,128)S(1)}, u32[]{:S(2)}, u32[]{:S(2)}) collective-permute-start(f32[64,1,6,512]{3,0,2,1:T(8,128)S(1)} %get-tuple-element.16), channel_id=1, source_target_pairs={{0,2},{1,3},{2,0},{3,1},{4,6},{5,7},{6,4},{7,5},{8,10},{9,11},{10,... | collective-permute-start | bytes 2359304 | tf_op jit(solution)/shard_map/ppermute | solution.py:84
  106.7 34.7 %collective-permute-start.2 = (f32[64,1,6,512]{3,0,2,1:T(8,128)S(1)}, f32[64,1,6,512]{3,0,2,1:T(8,128)S(1)}, u32[]{:S(2)}, u32[]{:S(2)}) collective-permute-start(f32[64,1,6,512]{3,0,2,1:T(8,128)S(1)} %get-tuple-element.15), channel_id=1, source_target_pairs={{0,3},{1,2},{2,1},{3,0},{4,7},{5,6},{6,5},{7,4},{8,11},{9,10},{10,... | collective-permute-start | bytes 2359304 | tf_op jit(solution)/shard_map/ppermute | solution.py:84
  106.9 54.8 %collective-permute-start.3 = (f32[64,1,6,512]{3,0,2,1:T(8,128)S(1)}, f32[64,1,6,512]{3,0,2,1:T(8,128)S(1)}, u32[]{:S(2)}, u32[]{:S(2)}) collective-permute-start(f32[64,1,6,512]{3,0,2,1:T(8,128)S(1)} %get-tuple-element.14), channel_id=1, source_target_pairs={{0,4},{1,5},{2,6},{3,7},{4,0},{5,1},{6,2},{7,3},{8,12},{9,13},{10,... | collective-permute-start | bytes 2359304 | tf_op jit(solution)/shard_map/ppermute | solution.py:84
  110.1 67.5 %collective-permute-start.4 = (f32[64,1,6,512]{3,0,2,1:T(8,128)S(1)}, f32[64,1,6,512]{3,0,2,1:T(8,128)S(1)}, u32[]{:S(2)}, u32[]{:S(2)}) collective-permute-start(f32[64,1,6,512]{3,0,2,1:T(8,128)S(1)} %get-tuple-element.13), channel_id=1, source_target_pairs={{0,5},{1,4},{2,7},{3,6},{4,1},{5,0},{6,3},{7,2},{8,13},{9,12},{10,... | collective-permute-start | bytes 2359304 | tf_op jit(solution)/shard_map/ppermute | solution.py:84
  111.1 67.5 %collective-permute-start.5 = (f32[64,1,6,512]{3,0,2,1:T(8,128)S(1)}, f32[64,1,6,512]{3,0,2,1:T(8,128)S(1)}, u32[]{:S(2)}, u32[]{:S(2)}) collective-permute-start(f32[64,1,6,512]{3,0,2,1:T(8,128)S(1)} %get-tuple-element.12), channel_id=1, source_target_pairs={{0,6},{1,7},{2,4},{3,5},{4,2},{5,3},{6,0},{7,1},{8,14},{9,15},{10,... | collective-permute-start | bytes 2359304 | tf_op jit(solution)/shard_map/ppermute | solution.py:84
  125.4 57.0 %collective-permute-start.6 = (f32[64,1,6,512]{3,0,2,1:T(8,128)S(1)}, f32[64,1,6,512]{3,0,2,1:T(8,128)S(1)}, u32[]{:S(2)}, u32[]{:S(2)}) collective-permute-start(f32[64,1,6,512]{3,0,2,1:T(8,128)S(1)} %get-tuple-element.11), channel_id=1, source_target_pairs={{0,7},{1,6},{2,5},{3,4},{4,3},{5,2},{6,1},{7,0},{8,15},{9,14},{10,... | collective-permute-start | bytes 2359304 | tf_op jit(solution)/shard_map/ppermute | solution.py:84
  200.3 10.8 %copy-start.8 = (f32[256]{0:T(256)S(1)}, f32[256]{0:T(256)}, u32[]{:S(2)}) copy-start(f32[256]{0:T(256)} %param.7) | copy-start | bytes 3076
  200.4 14.5 %copy-start.6 = (f32[512]{0:T(512)S(1)}, f32[512]{0:T(512)}, u32[]{:S(2)}) copy-start(f32[512]{0:T(512)} %param.8) | copy-start | bytes 6148
  200.4 107.5 %all-to-all-start.2 = ((f32[64,32,1,512]{3,0,2,1:T(8,128)}), f32[64,32,1,512]{3,0,2,1:T(8,128)}, u32[]{:S(2)}, u32[]{:S(2)}) async-start(f32[64,32,1,512]{3,0,2,1:T(8,128)} %fusion), calls=%async_computation.2 | async-start | bytes 8388608 | tf_op jit(solution)/shard_map/all_to_all | solution.py:124
  215.3 8.8 %copy-start.5 = (f32[1,2,512,512]{3,2,1,0:T(8,128)}, f32[1,2,512,512]{3,2,1,0:T(8,128)S(1)}, u32[]{:S(2)}) copy-start(f32[1,2,512,512]{3,2,1,0:T(8,128)S(1)} %broadcast_subtract_fusion) | copy-start | bytes 6291460
  224.1 7.0 %copy-start.2 = (f32[32,64,1,512]{3,1,0,2:T(8,128)}, f32[32,64,1,512]{3,1,0,2:T(8,128)S(1)}, u32[]{:S(2)}) copy-start(f32[32,64,1,512]{3,1,0,2:T(8,128)S(1)} %copy.24) | copy-start | bytes 12582916
  307.9 9.9 %copy-start.4 = (f32[2048,512]{1,0:T(8,128)S(1)}, f32[2048,512]{1,0:T(8,128)}, u32[]{:S(2)}) copy-start(f32[2048,512]{1,0:T(8,128)} %fusion.24) | copy-start | bytes 12582916
  434.3 4.4 %copy-start.1 = (f32[768,512]{1,0:T(8,128)S(1)}, f32[768,512]{1,0:T(8,128)}, u32[]{:S(2)}) copy-start(f32[768,512]{1,0:T(8,128)} %param.6) | copy-start | bytes 4718596
